TPU v7x, 32 devices: a whole 2x2x4 slice. The times are simulated.
32 devices in a mesh: bunch: 4 (over y, x), mp: 8 (over z, core).
Axes of the slice: x: 2, y: 2, z: 4, core: 2. Of those that a mesh axis runs over, the one named last changes fastest.
Arguments:
- phase_space: float32 [4, 64, 32768], P(None, 'bunch', 'mp')
- phase_advance: float32 [2, 64], P(None, 'bunch'), may hold values from 0.3 to 2.8
- centroid_history: float32 [2, 64, 64], P(None, None, 'bunch'), may hold values from -6 to 6
- lr_wake: float32 [4160], replicated, may hold values from -0.09375 to 0.09375
- sr_dipole: float32 [256, 256], replicated, may hold values from -24 to 24
- sr_quad: float32 [256, 256], replicated, may hold values from -24 to 24
- slice_ids: int32 [2, 64, 32768], P(None, 'bunch', 'mp'), may hold values from 0 to 255
Outputs:
- tracked: float32 [4, 64, 32768], P(None, 'bunch', 'mp')
- centroids: float32 [2, 2, 64], P(None, None, 'bunch')
All inputs are finite; a program needn't handle non-finite values.
Results may differ from a plain program's by a relative error of at most 0.00019.
Values sent between devices are 32-bit elements; how exact they have to be, the bound alone decides.
No kernel may reach another device: no remote copies, remote signals or barrier semaphores. Data moves between devices by JAX's collectives and lax.ppermute only.
A program may use at most 64 MiB of HBM per device.

v0:
```python
import jax
import jax.numpy as jnp
from jax import lax
from jax.sharding import PartitionSpec as P

SLICES = 256
TURNS = 2
DETUNE = 0.02


def body(phase_space, phase_advance, centroid_history, lr_wake, sr_dipole, sr_quad, slice_ids):
    highest = lax.Precision.HIGHEST
    bunch_dev = phase_space.shape[1]
    depth = centroid_history.shape[1]
    macro_total = phase_space.shape[2] * lax.axis_size("mp")
    all_bunches = bunch_dev * lax.axis_size("bunch")
    length = (depth + 1) * all_bunches
    offset_bunch = lax.axis_index("bunch") * bunch_dev
    own_index = jnp.arange(bunch_dev, dtype=jnp.int32)
    levels = jnp.arange(SLICES, dtype=jnp.int32)
    padded = jnp.concatenate([jnp.zeros((all_bunches,), jnp.float32), lr_wake])
    windows = jax.vmap(lambda start_at: lax.dynamic_slice(padded, (start_at,), (length,)))(
        offset_bunch + own_index
    )
    history = centroid_history
    whole = lax.all_gather(centroid_history, "bunch", axis=2, tiled=True)

    def moments_of(member):
        slice_line, line_x, line_y = member
        onehot = (slice_line[:, None] == levels[None, :]).astype(jnp.float32)
        stacked = jnp.stack([jnp.ones_like(line_x), line_x, line_y])
        return jnp.dot(stacked, onehot, precision=highest, preferred_element_type=jnp.float32)

    def lookup(member):
        slice_line, kick_rows = member
        onehot = (slice_line[:, None] == levels[None, :]).astype(jnp.float32)
        return lax.dot_general(
            kick_rows,
            onehot,
            (((1,), (1,)), ((), ())),
            precision=highest,
            preferred_element_type=jnp.float32,
        )

    coords = phase_space
    centroid_rows = []
    for turn_index in range(TURNS):
        slice_row = slice_ids[turn_index]
        moments = lax.map(moments_of, (slice_row, coords[0], coords[2]))
        moments = lax.psum(moments, "mp")
        density = moments[:, 0] / macro_total
        dipole = jnp.stack([moments[:, 1], moments[:, 2]]) / macro_total
        centroid = jnp.sum(dipole, axis=2)
        centroid_rows.append(centroid)
        dip_kick = jnp.einsum("pbj,ij->pbi", dipole, sr_dipole, precision=highest)
        quad_kick = jnp.einsum("bj,ij->bi", density, sr_quad, precision=highest)
        current_all = lax.all_gather(centroid, "bunch", axis=1, tiled=True)
        all_rows = jnp.concatenate([current_all[:, None, :], whole], axis=1)[:, :, ::-1].reshape(
            2, length
        )
        far_kick = jnp.einsum("bk,pk->pb", windows, all_rows, precision=highest)
        whole = jnp.concatenate([current_all[:, None, :], whole[:, :-1]], axis=1)
        kick_table = jnp.stack([dip_kick[0], dip_kick[1], quad_kick], axis=1)
        picked = lax.map(lookup, (slice_row, kick_table))
        coord_x, moment_x, coord_y, moment_y = (coords[0], coords[1], coords[2], coords[3])
        moment_x = moment_x + picked[:, 0] + picked[:, 2] * coord_x + far_kick[0][:, None]
        moment_y = moment_y + picked[:, 1] - picked[:, 2] * coord_y + far_kick[1][:, None]
        action = coord_x * coord_x + moment_x * moment_x + coord_y * coord_y + moment_y * moment_y
        angle_x = phase_advance[0][:, None] + DETUNE * action
        angle_y = phase_advance[1][:, None] + DETUNE * action
        new_x = jnp.cos(angle_x) * coord_x + jnp.sin(angle_x) * moment_x
        new_mx = -jnp.sin(angle_x) * coord_x + jnp.cos(angle_x) * moment_x
        new_y = jnp.cos(angle_y) * coord_y + jnp.sin(angle_y) * moment_y
        new_my = -jnp.sin(angle_y) * coord_y + jnp.cos(angle_y) * moment_y
        coords = jnp.stack([new_x, new_mx, new_y, new_my])
        history = jnp.concatenate([centroid[:, None, :], history[:, :-1]], axis=1)
    return (coords, jnp.stack(centroid_rows, axis=1))


def solution(mesh):
    placed = (
        P(None, "bunch", "mp"),
        P(None, "bunch"),
        P(None, None, "bunch"),
        P(),
        P(),
        P(),
        P(None, "bunch", "mp"),
    )
    return jax.shard_map(
        body,
        mesh=mesh,
        in_specs=placed,
        out_specs=(P(None, "bunch", "mp"), P(None, None, "bunch")),
        check_vma=False,
    )
```

profile of v0, /device:TPU:0, one launch (start us, length us, event | category | flops | bytes accessed | tf_op | source)
XLA Modules:
  0.0 306.1 jit_solution(7244623451006268379)
XLA Ops:
  1.6 9.9 %all_gather.10 = f32[2,64,64]{1,2,0:T(8,128)S(1)} all-gather(f32[2,64,16]{1,2,0:T(8,128)} %param.17), channel_id=1, replica_groups=mesh['bunch'=4,'mp'=8] {'bunch'}, dimensions={2}, use_global_device_ids=true | all-gather | bytes 40960 | tf_op jit(solution)/shard_map/all_gather | solution.py:26
  11.4 28.2 %while.45 = (s32[]{:T(128)}, f32[4224]{0:T(1024)S(1)}, s32[16,1]{0,1:T(1,128)S(1)}, f32[16,4160]{1,0:T(8,128)S(1)}, s32[]{:T(128)}, /*index=5*/s32[]{:T(128)}) while((s32[]{:T(128)}, f32[4224]{0:T(1024)S(1)}, s32[16,1]{0,1:T(1,128)S(1)}, f32[16,4160]{1,0:T(8,128)S(1)}, s32[]{:T(128)}, /*index=5*/s32[]{:T(128)}) %tuple.122), condition=%wide.while_cond, body=%wide.while_body.sunk | while | flops 2 | bytes 99937 | solution.py:22
  39.7 1.8 slice_bitcast_fusion
  41.5 25.6 %while.46 = (s32[]{:T(128)}, f32[16,3,256]{2,0,1:T(8,128)S(1)}, f32[16,4096]{1,0:T(8,128)S(1)}, f32[16,4096]{1,0:T(8,128)S(1)}, s32[16,4096]{1,0:T(8,128)S(1)}, ...) while((s32[]{:T(128)}, f32[16,3,256]{2,0,1:T(8,128)S(1)}, f32[16,4096]{1,0:T(8,128)S(1)}, ...), condition=%wide.region_1.2_spmd.clone, body=%wide.region_0.1_spmd.clone.sunk | while | flops 38821888 | bytes 162961 | solution.py:49
  41.6 1.4 fusion.77
  59.2 1.4 fusion.77
  67.1 27.5 %psum.14 = f32[16,3,256]{2,0,1:T(8,128)S(1)} all-reduce(f32[16,3,256]{2,0,1:T(8,128)S(1)} %get-tuple-element.120), channel_id=1, replica_groups=mesh['bunch'=4,'mp'=8] {'mp'}, use_global_device_ids=true, to_apply=%region_2.3 | all-reduce | flops 12288 | bytes 98304 | tf_op jit(solution)/shard_map/psum | solution.py:50
  95.5 7.7 %all-gather = f32[4,16,2]{1,2,0:T(2,128)S(1)} all-gather(f32[1,16,2]{1,2,0:T(2,128)S(1)} %bitcast.229), channel_id=1, replica_groups=mesh['bunch'=4,'mp'=8] {'bunch'}, dimensions={0}, use_global_device_ids=true | all-gather | bytes 640 | tf_op jit(solution)/shard_map/all_gather | solution.py:57
  104.2 42.7 %while.47 = (s32[]{:T(128)}, f32[16,3,4096]{2,0,1:T(8,128)S(1)}, f32[16,3,256]{2,0,1:T(8,128)S(1)}, s32[16,4096]{1,0:T(8,128)S(1)}, s32[]{:T(128)}, /*index=5*/s32[]{:T(128)}) while((s32[]{:T(128)}, f32[16,3,4096]{2,0,1:T(8,128)S(1)}, f32[16,3,256]{2,0,1:T(8,128)S(1)}, s32[16,4096]{1,0:T(8,128)S(1)}, s32[]{:T(128)}, ...), condition=%wide.region_4.5_spmd.clone, body=%wide.region_3.4_spmd.clone.sunk | while | flops 38797312 | bytes 304217 | solution.py:64
  104.3 2.1 convolution_bitcast_fusion.6
  107.0 2.1 convolution_bitcast_fusion.6
  109.6 2.1 convolution_bitcast_fusion.6
  112.3 2.1 convolution_bitcast_fusion.6
  115.0 2.1 convolution_bitcast_fusion.6
  117.6 2.1 convolution_bitcast_fusion.6
  120.3 2.1 convolution_bitcast_fusion.6
  123.0 2.1 convolution_bitcast_fusion.6
  125.7 2.1 convolution_bitcast_fusion.6
  128.3 2.1 convolution_bitcast_fusion.6
  131.0 2.1 convolution_bitcast_fusion.6
  133.7 2.1 convolution_bitcast_fusion.6
  136.3 2.1 convolution_bitcast_fusion.6
  139.0 2.1 convolution_bitcast_fusion.6
  141.7 2.1 convolution_bitcast_fusion.6
  144.3 2.1 convolution_bitcast_fusion.6
  147.0 3.1 %multiply_add_fusion.5 = (f32[16,4096]{1,0:T(8,128)}, f32[16,4096]{1,0:T(8,128)}) fusion(f32[16]{0:T(128)S(1)} %get-tuple-element.281, f32[16]{0:T(128)S(1)} %get-tuple-element.285, f32[16,3,4096]{2,0,1:T(8,128)S(1)} %get-tuple-element.121, f32[4,16,4096]{2,1,0:T(8,128)S(1)} %copy-done.1, f32[16]{0:T(128)S(1)} %get-tuple-element.286, ...), kind=kLoop, calls=%fused_computation.81 | loop fusion | flops 1572864 | bytes 2359552 | tf_op jit(solution)/shard_map/add | solution.py:73
  150.9 55.3 %while.48 = (s32[]{:T(128)}, f32[16,3,256]{2,0,1:T(8,128)S(1)}, f32[16,4096]{1,0:T(8,128)}, f32[16,4096]{1,0:T(8,128)}, s32[16,4096]{1,0:T(8,128)}, /*index=5*/s32[]{:T(128)}, f32[]{:T(128)}, f32[]{:T(128)}, s32[]{:T(128)}) while((s32[]{:T(128)}, f32[16,3,256]{2,0,1:T(8,128)S(1)}, f32[16,4096]{1,0:T(8,128)}, f32[16,4096]{1,0:T(8,128)}, ...), condition=%wide.region_7.8_spmd.clone, body=%wide.region_6.7_spmd.clone.sunk | while | flops 38821888 | bytes 162961 | solution.py:49
  206.3 26.3 %psum.15 = f32[16,3,256]{2,0,1:T(8,128)S(1)} all-reduce(f32[16,3,256]{2,0,1:T(8,128)S(1)} %get-tuple-element.122), channel_id=1, replica_groups=mesh['bunch'=4,'mp'=8] {'mp'}, use_global_device_ids=true, to_apply=%region_8.9 | all-reduce | flops 12288 | bytes 98304 | tf_op jit(solution)/shard_map/psum | solution.py:50
  234.0 7.5 %all-gather.1 = f32[4,16,2]{1,2,0:T(2,128)S(1)} all-gather(f32[1,16,2]{1,2,0:T(2,128)S(1)} %bitcast.232), channel_id=1, replica_groups=mesh['bunch'=4,'mp'=8] {'bunch'}, dimensions={0}, use_global_device_ids=true | all-gather | bytes 640 | tf_op jit(solution)/shard_map/all_gather | solution.py:57
  242.5 57.1 %while.49 = (s32[]{:T(128)}, f32[16,3,4096]{2,0,1:T(8,128)S(1)}, f32[16,3,256]{2,0,1:T(8,128)S(1)}, s32[16,4096]{1,0:T(8,128)}, s32[]{:T(128)}, /*index=5*/s32[]{:T(128)}) while((s32[]{:T(128)}, f32[16,3,4096]{2,0,1:T(8,128)S(1)}, f32[16,3,256]{2,0,1:T(8,128)S(1)}, s32[16,4096]{1,0:T(8,128)}, s32[]{:T(128)}, ...), condition=%wide.region_10.11_spmd.clone, body=%wide.region_9.10_spmd.clone.sunk | while | flops 38797312 | bytes 304217 | solution.py:64
  243.5 2.1 convolution_bitcast_fusion.7
  247.0 2.1 convolution_bitcast_fusion.7
  250.6 2.1 convolution_bitcast_fusion.7
  254.2 2.1 convolution_bitcast_fusion.7
  257.8 2.1 convolution_bitcast_fusion.7
  261.3 2.1 convolution_bitcast_fusion.7
  264.9 2.1 convolution_bitcast_fusion.7
  268.5 2.1 convolution_bitcast_fusion.7
  272.0 2.1 convolution_bitcast_fusion.7
  275.6 2.1 convolution_bitcast_fusion.7
  279.2 2.1 convolution_bitcast_fusion.7
  282.7 2.1 convolution_bitcast_fusion.7
  286.3 2.1 convolution_bitcast_fusion.7
  289.9 2.1 convolution_bitcast_fusion.7
  293.4 2.1 convolution_bitcast_fusion.7
  297.0 2.1 convolution_bitcast_fusion.7
  299.6 3.3 %multiply_add_fusion.3 = (f32[1,16,4096]{2,1,0:T(8,128)S(1)}, f32[1,16,4096]{2,1,0:T(8,128)S(1)}, f32[1,16,4096]{2,1,0:T(8,128)S(1)}, f32[1,16,4096]{2,1,0:T(8,128)S(1)}, f32[1,16,4096]{2,1,0:T(8,128)S(1)}) fusion(f32[16]{0:T(128)S(1)} %copy-done.4, f32[16]{0:T(128)S(1)} %get-tuple-element.280, f32[16,3,4096]{2,0,1:T(8,128)S(1)} %get-tuple-element.123, ...), kind=kLoop, calls=%fused_computation.77 | loop fusion | flops 2359296 | bytes 3408128 | tf_op jit(solution)/shard_map/add | solution.py:71
  302.9 2.2 multiply_add_fusion.1
  (440 shorter events, 141.8 us)
Async XLA Ops:
  0.6 94.5 %copy-start = (f32[256,256]{1,0:T(8,128)S(1)}, f32[256,256]{1,0:T(8,128)}, u32[]{:S(2)}) copy-start(f32[256,256]{1,0:T(8,128)} %param.19) | copy-start | bytes 786436
  0.6 40.8 %copy-start.1 = (f32[4,16,4096]{2,1,0:T(8,128)S(1)}, f32[4,16,4096]{2,1,0:T(8,128)}, u32[]{:S(2)}) copy-start(f32[4,16,4096]{2,1,0:T(8,128)} %param.15) | copy-start | bytes 3145732
  41.5 53.2 %copy-start.2 = (f32[256,256]{1,0:T(8,128)S(1)}, f32[256,256]{1,0:T(8,128)}, u32[]{:S(2)}) copy-start(f32[256,256]{1,0:T(8,128)} %param.20) | copy-start | bytes 786436
  67.1 37.0 %copy-start.7 = (f32[2,16]{1,0:T(2,128)S(1)}, f32[2,16]{1,0:T(2,128)}, u32[]{:S(2)}) copy-start(f32[2,16]{1,0:T(2,128)} %param.16) | copy-start | bytes 388
  104.1 42.8 %copy-start.3 = (f32[16]{0:T(128)}, f32[16]{0:T(128)S(1)}, u32[]{:S(2)}) copy-start(f32[16]{0:T(128)S(1)} %get-tuple-element.282) | copy-start | bytes 196
  104.2 42.8 %copy-start.5 = (f32[16]{0:T(128)}, f32[16]{0:T(128)S(1)}, u32[]{:S(2)}) copy-start(f32[16]{0:T(128)S(1)} %get-tuple-element.285) | copy-start | bytes 196
  104.2 42.8 %copy-start.6 = (f32[16]{0:T(128)}, f32[16]{0:T(128)S(1)}, u32[]{:S(2)}) copy-start(f32[16]{0:T(128)S(1)} %get-tuple-element.286) | copy-start | bytes 196
  242.5 57.1 %copy-start.4 = (f32[16]{0:T(128)S(1)}, f32[16]{0:T(128)}, u32[]{:S(2)}) copy-start(f32[16]{0:T(128)} %copy-done.3) | copy-start | bytes 196
where the time goes:
time: 307 us; the launch traced here: 306 us
  matrix products  116 us (38%)
  local copies, waits for them, and re-layouts  95.8 us (31%)
  blocking collectives  78.9 us (26%)
  other arithmetic  10.8 us (4%)
  loops' own time  3.22 us (1%)
    dot_general x32, matrix products, lookup(): lax.dot_general(kick_rows, onehot, (((1,), (1,)), ((), ())), precision=hi...  68 us
    psum x2, blocking collectives, body(): moments = lax.psum(moments, 'mp')  53.9 us
    dynamic_slice x96, local copies, waits for them, and re-layouts, body(): moments = lax.map(moments_of, (slice_row, coords[0], coords[2]))  46.8 us
    dot_general x32, matrix products, moments_of(): jnp.dot(stacked, onehot, precision=highest, preferred_element_type=jnp.fl...  46.3 us
    gather x64, local copies, waits for them, and re-layouts  27.8 us
    all_gather x2, blocking collectives, body(): current_all = lax.all_gather(centroid, 'bunch', axis=1, tiled=True)  15.2 us
    dynamic_update_slice x64, local copies, waits for them, and re-layouts, body(): picked = lax.map(lookup, (slice_row, kick_table))  14.9 us
    all_gather x1, blocking collectives, body(): whole = lax.all_gather(centroid_history, 'bunch', axis=2, tiled=True)  9.87 us

commit v1 on v0

--- a/solution.py
+++ b/solution.py
@@ -6,6 +6,14 @@
 SLICES = 256
 TURNS = 2
 DETUNE = 0.02
+
+
+def added_up(shard, axis):
+    peers, result = (lax.axis_size(axis), shard)
+    for far in [1 << k for k in range(peers.bit_length() - 1)]:
+        pairs = [(i, i ^ far) for i in range(peers)]
+        result = result + lax.ppermute(result, axis, pairs)
+    return result
 
 
 def body(phase_space, phase_advance, centroid_history, lr_wake, sr_dipole, sr_quad, slice_ids):
@@ -47,7 +55,7 @@
     for turn_index in range(TURNS):
         slice_row = slice_ids[turn_index]
         moments = lax.map(moments_of, (slice_row, coords[0], coords[2]))
-        moments = lax.psum(moments, "mp")
+        moments = added_up(moments, "mp")
         density = moments[:, 0] / macro_total
         dipole = jnp.stack([moments[:, 1], moments[:, 2]]) / macro_total
         centroid = jnp.sum(dipole, axis=2)

time: 307 us -> 241 us (0.79)
  blocking collectives: 78.9 us -> 23.6 us
  local copies, waits for them, and re-layouts: 95.8 us -> 66.9 us
  waiting for transfers between devices: 0 us -> 11.1 us
  starting transfers between devices: 0 us -> 8.75 us
    psum x2 -> x0, blocking collectives: 53.9 us -> none  [body(): moments = lax.psum(moments, 'mp')]
    dynamic_slice x96, local copies, waits for them, and re-layouts: 46.8 us -> 16.9 us  [body(): moments = lax.map(moments_of, (slice_row, coords[0], coords[2]))]
    ppermute x0 -> x6, waiting for transfers between devices: none -> 11.1 us  [added_up(): result = result + lax.ppermute(result, axis, pairs)]
    ppermute x0 -> x6, starting transfers between devices: none -> 8.75 us  [added_up(): result = result + lax.ppermute(result, axis, pairs)]
  transfers between devices with their start and end apart: 0 -> 6, of which waited for: 0 -> 5; matrix products, arithmetic and copies ran while one was open for 0% -> 12% of each run, Pallas kernels for 0% -> 0%
where the time goes in v1:
time: 241 us; the launch traced here: 240 us
  matrix products  116 us (48%)
  local copies, waits for them, and re-layouts  66.9 us (28%)
  blocking collectives  23.6 us (10%)
  waiting for transfers between devices  11.1 us (5%)
  other arithmetic  9.41 us (4%)
  starting transfers between devices  8.75 us (4%)
  loops' own time  3.35 us (1%)
    dot_general x32, matrix products, lookup(): lax.dot_general(kick_rows, onehot, (((1,), (1,)), ((), ())), precision=hi...  68 us
    dot_general x32, matrix products, moments_of(): jnp.dot(stacked, onehot, precision=highest, preferred_element_type=jnp.fl...  46.3 us
    gather x64, local copies, waits for them, and re-layouts  29.6 us
    dynamic_slice x96, local copies, waits for them, and re-layouts, body(): moments = lax.map(moments_of, (slice_row, coords[0], coords[2]))  16.9 us
    all_gather x2, blocking collectives, body(): current_all = lax.all_gather(centroid, 'bunch', axis=1, tiled=True)  15.3 us
    dynamic_update_slice x64, local copies, waits for them, and re-layouts, body(): picked = lax.map(lookup, (slice_row, kick_table))  15.1 us
    ppermute x6, waiting for transfers between devices, added_up(): result = result + lax.ppermute(result, axis, pairs)  11.1 us
    ppermute x6, starting transfers between devices, added_up(): result = result + lax.ppermute(result, axis, pairs)  8.75 us
  transfers between devices with their start and end apart: 6, of which 5 were waited for; matrix products, arithmetic and copies ran while one was open for 12% of the time, Pallas kernels for 0%

profile of v1, /device:TPU:0, one launch (start us, length us, event | category | flops | bytes accessed | tf_op | source)
XLA Modules:
  0.0 240.5 jit_solution(1176435010347008344)
XLA Ops:
  2.1 25.6 %while.46 = (s32[]{:T(128)}, f32[16,3,256]{2,0,1:T(8,128)S(1)}, f32[16,4096]{1,0:T(8,128)S(1)}, f32[16,4096]{1,0:T(8,128)S(1)}, s32[16,4096]{1,0:T(8,128)S(1)}, ...) while((s32[]{:T(128)}, f32[16,3,256]{2,0,1:T(8,128)S(1)}, f32[16,4096]{1,0:T(8,128)S(1)}, ...), condition=%wide.region_1.2_spmd.clone, body=%wide.region_0.1_spmd.clone.sunk | while | flops 38821888 | bytes 162961 | solution.py:57
  29.2 3.0 %collective-permute-start.1 = (f32[16,3,256]{2,0,1:T(8,128)S(1)}, f32[16,3,256]{2,0,1:T(8,128)S(1)}, u32[]{:S(2)}, u32[]{:S(2)}) collective-permute-start(f32[16,3,256]{2,0,1:T(8,128)S(1)} %add.306), channel_id=1, source_target_pairs={{0,2},{1,3},{2,0},{3,1},{4,6},{5,7},{6,4},{7,5},{8,10},{9,11},{10,... | collective-permute-start | bytes 147464 | tf_op jit(solution)/shard_map/ppermute | solution.py:15
  32.2 2.1 collective-permute-done.1
  34.3 3.1 %collective-permute-start.2 = (f32[16,3,256]{2,0,1:T(8,128)S(1)}, f32[16,3,256]{2,0,1:T(8,128)S(1)}, u32[]{:S(2)}, u32[]{:S(2)}) collective-permute-start(f32[16,3,256]{2,0,1:T(8,128)S(1)} %add.307), channel_id=1, source_target_pairs={{0,4},{1,5},{2,6},{3,7},{4,0},{5,1},{6,2},{7,3},{8,12},{9,13},{10,... | collective-permute-start | bytes 147464 | tf_op jit(solution)/shard_map/ppermute | solution.py:15
  37.4 8.3 %all_gather.10 = f32[2,64,64]{1,2,0:T(8,128)S(1)} all-gather(f32[2,64,16]{1,2,0:T(8,128)S(1)} %copy-done.7), channel_id=1, replica_groups=mesh['bunch'=4,'mp'=8] {'bunch'}, dimensions={2}, use_global_device_ids=true | all-gather | bytes 40960 | tf_op jit(solution)/shard_map/all_gather | solution.py:34
  45.7 30.0 %while.45 = (s32[]{:T(128)}, f32[4224]{0:T(1024)S(1)}, s32[16,1]{0,1:T(1,128)S(1)}, f32[16,4160]{1,0:T(8,128)S(1)}, s32[]{:T(128)}, /*index=5*/s32[]{:T(128)}) while((s32[]{:T(128)}, f32[4224]{0:T(1024)S(1)}, s32[16,1]{0,1:T(1,128)S(1)}, f32[16,4160]{1,0:T(8,128)S(1)}, s32[]{:T(128)}, /*index=5*/s32[]{:T(128)}) %tuple.122), condition=%wide.while_cond, body=%wide.while_body.sunk | while | flops 2 | bytes 99937 | solution.py:30
  76.6 8.0 %all-gather = f32[4,16,2]{1,2,0:T(2,128)S(1)} all-gather(f32[1,16,2]{1,2,0:T(2,128)S(1)} %bitcast.229), channel_id=1, replica_groups=mesh['bunch'=4,'mp'=8] {'bunch'}, dimensions={0}, use_global_device_ids=true | all-gather | bytes 640 | tf_op jit(solution)/shard_map/all_gather | solution.py:65
  85.4 42.8 %while.47 = (s32[]{:T(128)}, f32[16,3,4096]{2,0,1:T(8,128)S(1)}, f32[16,3,256]{2,0,1:T(8,128)S(1)}, s32[16,4096]{1,0:T(8,128)S(1)}, s32[]{:T(128)}, /*index=5*/s32[]{:T(128)}) while((s32[]{:T(128)}, f32[16,3,4096]{2,0,1:T(8,128)S(1)}, f32[16,3,256]{2,0,1:T(8,128)S(1)}, s32[16,4096]{1,0:T(8,128)S(1)}, s32[]{:T(128)}, ...), condition=%wide.region_3.4_spmd.clone, body=%wide.region_2.3_spmd.clone.sunk | while | flops 38797312 | bytes 304217 | solution.py:72
  85.4 2.1 convolution_bitcast_fusion.6
  88.1 2.1 convolution_bitcast_fusion.6
  90.8 2.1 convolution_bitcast_fusion.6
  93.5 2.1 convolution_bitcast_fusion.6
  96.2 2.1 convolution_bitcast_fusion.6
  98.8 2.1 convolution_bitcast_fusion.6
  101.5 2.1 convolution_bitcast_fusion.6
  104.2 2.1 convolution_bitcast_fusion.6
  106.9 2.1 convolution_bitcast_fusion.6
  109.5 2.1 convolution_bitcast_fusion.6
  112.2 2.1 convolution_bitcast_fusion.6
  114.9 2.1 convolution_bitcast_fusion.6
  117.6 2.1 convolution_bitcast_fusion.6
  120.3 2.1 convolution_bitcast_fusion.6
  122.9 2.1 convolution_bitcast_fusion.6
  125.6 2.1 convolution_bitcast_fusion.6
  128.7 2.2 multiply_add_fusion.5
  130.9 25.6 %while.48 = (s32[]{:T(128)}, f32[16,3,256]{2,0,1:T(8,128)S(1)}, f32[16,4096]{1,0:T(8,128)S(1)}, f32[16,4096]{1,0:T(8,128)S(1)}, s32[16,4096]{1,0:T(8,128)S(1)}, ...) while((s32[]{:T(128)}, f32[16,3,256]{2,0,1:T(8,128)S(1)}, f32[16,4096]{1,0:T(8,128)S(1)}, ...), condition=%wide.region_6.7_spmd.clone, body=%wide.region_5.6_spmd.clone.sunk | while | flops 38821888 | bytes 162961 | solution.py:57
  159.4 2.5 %collective-permute-done.4 = f32[16,3,256]{2,0,1:T(8,128)S(1)} collective-permute-done((f32[16,3,256]{2,0,1:T(8,128)S(1)}, f32[16,3,256]{2,0,1:T(8,128)S(1)}, u32[]{:S(2)}, u32[]{:S(2)}) %collective-permute-start.4) | collective-permute-done | bytes 49184 | tf_op jit(solution)/shard_map/ppermute | solution.py:15
  162.6 4.4 %collective-permute-done.5 = f32[16,3,256]{2,0,1:T(8,128)S(1)} collective-permute-done((f32[16,3,256]{2,0,1:T(8,128)S(1)}, f32[16,3,256]{2,0,1:T(8,128)S(1)}, u32[]{:S(2)}, u32[]{:S(2)}) %collective-permute-start.5) | collective-permute-done | bytes 49184 | tf_op jit(solution)/shard_map/ppermute | solution.py:15
  168.4 7.3 %all-gather.1 = f32[4,16,2]{1,2,0:T(2,128)S(1)} all-gather(f32[1,16,2]{1,2,0:T(2,128)S(1)} %bitcast.232), channel_id=1, replica_groups=mesh['bunch'=4,'mp'=8] {'bunch'}, dimensions={0}, use_global_device_ids=true | all-gather | bytes 640 | tf_op jit(solution)/shard_map/all_gather | solution.py:65
  176.8 57.2 %while.49 = (s32[]{:T(128)}, f32[16,3,4096]{2,0,1:T(8,128)S(1)}, f32[16,3,256]{2,0,1:T(8,128)S(1)}, s32[16,4096]{1,0:T(8,128)}, s32[]{:T(128)}, /*index=5*/s32[]{:T(128)}) while((s32[]{:T(128)}, f32[16,3,4096]{2,0,1:T(8,128)S(1)}, f32[16,3,256]{2,0,1:T(8,128)S(1)}, s32[16,4096]{1,0:T(8,128)}, s32[]{:T(128)}, ...), condition=%wide.region_8.9_spmd.clone, body=%wide.region_7.8_spmd.clone.sunk | while | flops 38797312 | bytes 304217 | solution.py:72
  177.7 2.1 convolution_bitcast_fusion.7
  181.3 2.1 convolution_bitcast_fusion.7
  184.9 2.1 convolution_bitcast_fusion.7
  188.4 2.1 convolution_bitcast_fusion.7
  192.0 2.1 convolution_bitcast_fusion.7
  195.6 2.1 convolution_bitcast_fusion.7
  199.2 2.1 convolution_bitcast_fusion.7
  202.7 2.1 convolution_bitcast_fusion.7
  206.3 2.1 convolution_bitcast_fusion.7
  209.9 2.1 convolution_bitcast_fusion.7
  213.5 2.1 convolution_bitcast_fusion.7
  217.0 2.1 convolution_bitcast_fusion.7
  220.6 2.1 convolution_bitcast_fusion.7
  224.2 2.1 convolution_bitcast_fusion.7
  227.8 2.1 convolution_bitcast_fusion.7
  231.4 2.1 convolution_bitcast_fusion.7
  234.0 3.3 %multiply_add_fusion.3 = (f32[1,16,4096]{2,1,0:T(8,128)S(1)}, f32[1,16,4096]{2,1,0:T(8,128)S(1)}, f32[1,16,4096]{2,1,0:T(8,128)S(1)}, f32[1,16,4096]{2,1,0:T(8,128)S(1)}, f32[1,16,4096]{2,1,0:T(8,128)S(1)}) fusion(f32[16]{0:T(128)S(1)} %get-tuple-element.282, f32[16]{0:T(128)S(1)} %get-tuple-element.280, f32[16,3,4096]{2,0,1:T(8,128)S(1)} %get-tuple-element.123, ...), kind=kLoop, calls=%fused_computation.77 | loop fusion | flops 2359296 | bytes 3408128 | tf_op jit(solution)/shard_map/add | solution.py:79
  237.3 2.2 multiply_add_fusion.1
  (458 shorter events, 121.8 us)
Async XLA Ops:
  0.6 75.6 %copy-start = (f32[256,256]{1,0:T(8,128)S(1)}, f32[256,256]{1,0:T(8,128)}, u32[]{:S(2)}) copy-start(f32[256,256]{1,0:T(8,128)} %param.19) | copy-start | bytes 786436
  0.6 1.4 copy-start.1
  2.1 35.2 %copy-start.6 = (f32[4160]{0:T(1024)S(1)}, f32[4160]{0:T(1024)}, u32[]{:S(2)}) copy-start(f32[4160]{0:T(1024)} %param.18) | copy-start | bytes 49924
  2.1 35.3 %copy-start.7 = (f32[2,64,16]{1,2,0:T(8,128)S(1)}, f32[2,64,16]{1,2,0:T(8,128)}, u32[]{:S(2)}) copy-start(f32[2,64,16]{1,2,0:T(8,128)} %param.17) | copy-start | bytes 24580
  27.7 48.0 %copy-start.2 = (f32[256,256]{1,0:T(8,128)S(1)}, f32[256,256]{1,0:T(8,128)}, u32[]{:S(2)}) copy-start(f32[256,256]{1,0:T(8,128)} %param.20) | copy-start | bytes 786436
  27.7 1.4 collective-permute-start
  29.2 5.0 %collective-permute-start.1 = (f32[16,3,256]{2,0,1:T(8,128)S(1)}, f32[16,3,256]{2,0,1:T(8,128)S(1)}, u32[]{:S(2)}, u32[]{:S(2)}) collective-permute-start(f32[16,3,256]{2,0,1:T(8,128)S(1)} %add.306), channel_id=1, source_target_pairs={{0,2},{1,3},{2,0},{3,1},{4,6},{5,7},{6,4},{7,5},{8,10},{9,11},{10,... | collective-permute-start | bytes 147464 | tf_op jit(solution)/shard_map/ppermute | solution.py:15
  34.3 41.5 %collective-permute-start.2 = (f32[16,3,256]{2,0,1:T(8,128)S(1)}, f32[16,3,256]{2,0,1:T(8,128)S(1)}, u32[]{:S(2)}, u32[]{:S(2)}) collective-permute-start(f32[16,3,256]{2,0,1:T(8,128)S(1)} %add.307), channel_id=1, source_target_pairs={{0,4},{1,5},{2,6},{3,7},{4,0},{5,1},{6,2},{7,3},{8,12},{9,13},{10,... | collective-permute-start | bytes 147464 | tf_op jit(solution)/shard_map/ppermute | solution.py:15
  84.8 0.6 copy-start.4
  85.2 43.4 %copy-start.8 = (f32[2,16]{1,0:T(2,128)S(1)}, f32[2,16]{1,0:T(2,128)}, u32[]{:S(2)}) copy-start(f32[2,16]{1,0:T(2,128)} %param.16) | copy-start | bytes 388
  156.5 5.5 %copy-start.3 = (s32[16,4096]{1,0:T(8,128)}, s32[16,4096]{1,0:T(8,128)S(1)}, u32[]{:S(2)}) copy-start(s32[16,4096]{1,0:T(8,128)S(1)} %get-tuple-element.540) | copy-start | bytes 786436
  156.5 1.3 collective-permute-start.3
  157.8 4.2 %collective-permute-start.4 = (f32[16,3,256]{2,0,1:T(8,128)S(1)}, f32[16,3,256]{2,0,1:T(8,128)S(1)}, u32[]{:S(2)}, u32[]{:S(2)}) collective-permute-start(f32[16,3,256]{2,0,1:T(8,128)S(1)} %add.342), channel_id=1, source_target_pairs={{0,2},{1,3},{2,0},{3,1},{4,6},{5,7},{6,4},{7,5},{8,10},{9,11},{10,... | collective-permute-start | bytes 147464 | tf_op jit(solution)/shard_map/ppermute | solution.py:15
  162.0 5.1 %collective-permute-start.5 = (f32[16,3,256]{2,0,1:T(8,128)S(1)}, f32[16,3,256]{2,0,1:T(8,128)S(1)}, u32[]{:S(2)}, u32[]{:S(2)}) collective-permute-start(f32[16,3,256]{2,0,1:T(8,128)S(1)} %add.343), channel_id=1, source_target_pairs={{0,4},{1,5},{2,6},{3,7},{4,0},{5,1},{6,2},{7,3},{8,12},{9,13},{10,... | collective-permute-start | bytes 147464 | tf_op jit(solution)/shard_map/ppermute | solution.py:15
  162.6 13.3 %copy-start.5 = (f32[2,1,64]{1,2,0:T(8,128)S(1)}, f32[2,1,64]{1,2,0:T(8,128)}, u32[]{:S(2)}) copy-start(f32[2,1,64]{1,2,0:T(8,128)} %copy-done.4) | copy-start | bytes 1540
